TPU v7x, 128 devices: a whole 4x4x4 slice. The times are simulated.
128 devices in a mesh: patch: 16 (over z, x_lo, core), head: 8 (over y, x_hi).
Axes of the slice: x: 4 (x_hi: 2, x_lo: 2; x = x_hi * 2 + x_lo), y: 4, z: 4, core: 2. Of those that a mesh axis runs over, the one named last changes fastest.
Arguments:
- img_qkv: bfloat16 [8192, 9216], P(('patch', 'head')), may hold values from -8 to 8
- txt_qkv: bfloat16 [512, 9216], P('head'), may hold values from -8 to 8
- stale_kv: bfloat16 [2, 8192, 3072], P(None, 'patch', 'head'), may hold values from -8 to 8
- residual: bfloat16 [8192, 3072], P(('patch', 'head')), may hold values from -4 to 4
- gate_scale: float32 [3072], replicated, may hold values from 0.5 to 3
- proj_weight: bfloat16 [3072, 3072], replicated, may hold values from -0.109375 to 0.109375
Outputs:
- image_out: bfloat16 [8192, 3072], P(('patch', 'head'))
- text_attn: bfloat16 [512, 3072], P('head')
All inputs are finite; a program needn't handle non-finite values.
Results may differ from a plain program's by a relative error of at most 0.0075.
Values may be sent and summed in bfloat16 or wider, within the bound.
A program may use at most 192 MiB of HBM per device.

v0:
```python
import math

import jax
import jax.numpy as jnp
from jax import lax
from jax.sharding import PartitionSpec as P

HD = 128


def block_stats(queries, key_rows, values):
    scores = jnp.einsum("rhd,khd->rhk", queries, key_rows, preferred_element_type=jnp.float32) * (
        1.0 / math.sqrt(HD)
    )
    row_max = jnp.max(scores, axis=2)
    shifted = jnp.exp(scores - row_max[:, :, None])
    row_sum = jnp.sum(shifted, axis=2)
    weighted = jnp.einsum(
        "rhk,khd->rhd", shifted.astype(jnp.bfloat16), values, preferred_element_type=jnp.float32
    )
    return (row_max, row_sum, weighted)


def combine(first, second):
    joint_max = jnp.maximum(first[0], second[0])
    first_scale = jnp.exp(first[0] - joint_max)
    second_scale = jnp.exp(second[0] - joint_max)
    return (
        joint_max,
        first[1] * first_scale + second[1] * second_scale,
        first[2] * first_scale[:, :, None] + second[2] * second_scale[:, :, None],
    )


def finish(totals):
    return (totals[2] / totals[1][:, :, None]).astype(jnp.bfloat16)


def per_device(img_qkv, txt_qkv, stale_kv, residual, gate_scale, proj_weight):
    my_group = lax.axis_index("patch")
    img_rows = img_qkv.shape[0]
    model_width = img_qkv.shape[1] // 3
    head_count = model_width // HD
    img_split = img_qkv.reshape(img_rows, 3, head_count, HD)
    txt_split = txt_qkv.reshape(txt_qkv.shape[0], 3, head_count, HD)
    img_heads, txt_heads = (
        lax.all_to_all(img_split, "head", split_axis=2, concat_axis=0, tiled=True),
        lax.all_to_all(txt_split, "head", split_axis=2, concat_axis=0, tiled=True),
    )
    query_img = img_heads[:, 0]
    keys_img = img_heads[:, 1]
    values_img = img_heads[:, 2]
    query_txt = txt_heads[:, 0]
    keys_txt = txt_heads[:, 1]
    values_txt = txt_heads[:, 2]
    group_rows = query_img.shape[0]
    local_heads = query_img.shape[1]
    image_init = block_stats(query_img, keys_txt, values_txt)
    text_init = block_stats(query_txt, keys_txt, values_txt)
    own_first = my_group * group_rows
    shard_rows = lax.all_gather(stale_kv, "patch", axis=1, tiled=True)
    shard_count = shard_rows.shape[1] // group_rows
    key_blocks = jnp.moveaxis(shard_rows.reshape(2, shard_count, group_rows, local_heads, HD), 1, 0)
    starts = group_rows * jnp.arange(shard_count, dtype=jnp.int32)

    def one_block(running_pair, inputs):
        key_block, block_first = inputs
        is_fresh = block_first == own_first
        key_rows = jnp.where(is_fresh, keys_img, key_block[0])
        values = jnp.where(is_fresh, values_img, key_block[1])
        image_next = combine(running_pair[0], block_stats(query_img, key_rows, values))
        text_next = combine(running_pair[1], block_stats(query_txt, key_block[0], key_block[1]))
        return ((image_next, text_next), None)

    result, _ = lax.scan(one_block, (image_init, text_init), (key_blocks, starts))
    image_total, text_total = result
    image_attn = finish(image_total)
    text_attn = finish(text_total)
    image_back, text_back = (
        lax.all_to_all(image_attn, "head", split_axis=0, concat_axis=1, tiled=True),
        lax.all_to_all(text_attn, "head", split_axis=0, concat_axis=1, tiled=True),
    )
    image_flat = image_back.reshape(img_rows, model_width)
    projected = jnp.dot(image_flat, proj_weight, preferred_element_type=jnp.float32)
    image_out = (residual.astype(jnp.float32) + gate_scale * projected).astype(jnp.bfloat16)
    return (image_out, text_back.reshape(text_back.shape[0], model_width))


def solution(mesh):
    return jax.shard_map(
        per_device,
        mesh=mesh,
        in_specs=(
            P(("patch", "head"), None),
            P("head", None),
            P(None, "patch", "head"),
            P(("patch", "head"), None),
            P(),
            P(),
        ),
        out_specs=(P(("patch", "head"), None), P("head", None)),
        check_vma=False,
    )
```

profile of v0, /device:TPU:96, one launch (start us, length us, event | category | flops | bytes accessed | tf_op | source)
XLA Modules:
  0.0 355.6 jit_solution(2656296785264345013)
XLA Ops:
  10.8 6.9 %all-to-all-start.1 = ((bf16[64,3,24,128]{3,0,1,2:T(8,128)(2,1)}), bf16[64,3,24,128]{3,0,1,2:T(8,128)(2,1)S(1)}, u32[]{:S(2)}, u32[]{:S(2)}) async-start(bf16[64,3,24,128]{3,0,1,2:T(8,128)(2,1)} %copy.82), calls=%async_computation.1 | async-start | bytes 2359296 | tf_op jit(solution)/shard_map/all_to_all | solution.py:47
  19.3 29.1 %all-to-all-done.1 = bf16[64,3,24,128]{3,0,1,2:T(8,128)(2,1)S(1)} async-done(((bf16[64,3,24,128]{3,0,1,2:T(8,128)(2,1)}), bf16[64,3,24,128]{3,0,1,2:T(8,128)(2,1)S(1)}, u32[]{:S(2)}, u32[]{:S(2)}) %all-to-all-start.1) | async-done | bytes 1179680 | tf_op jit(solution)/shard_map/all_to_all | solution.py:47
  48.3 4.3 %all-to-all-start = ((bf16[64,3,24,128]{3,0,1,2:T(8,128)(2,1)}), bf16[64,3,24,128]{3,0,1,2:T(8,128)(2,1)}, u32[]{:S(2)}, u32[]{:S(2)}) async-start(bf16[64,3,24,128]{3,0,1,2:T(8,128)(2,1)} %copy.79), calls=%async_computation | async-start | bytes 2359296 | tf_op jit(solution)/shard_map/all_to_all | solution.py:48
  52.7 30.9 %all-to-all-done = bf16[64,3,24,128]{3,0,1,2:T(8,128)(2,1)} async-done(((bf16[64,3,24,128]{3,0,1,2:T(8,128)(2,1)}), bf16[64,3,24,128]{3,0,1,2:T(8,128)(2,1)}, u32[]{:S(2)}, u32[]{:S(2)}) %all-to-all-start) | async-done | bytes 1179680 | tf_op jit(solution)/shard_map/all_to_all | solution.py:48
  94.2 2.9 fusion.49
  97.2 7.7 %all-gather.2.cloned.1.call-done = bf16[2,8192,384]{2,1,0:T(8,128)(2,1)} async-done(((bf16[2,512,384]{2,1,0:T(8,128)(2,1)}), bf16[2,8192,384]{2,1,0:T(8,128)(2,1)}) %all-gather.2.cloned.1.call-update) | async-done | bytes 12582928 | tf_op jit(solution)/shard_map/all_gather | solution.py:61
  104.9 16.7 %copy.87 = bf16[2,8192,384]{1,2,0:T(8,128)(2,1)} copy(bf16[2,8192,384]{2,1,0:T(8,128)(2,1)} %all-gather.2.cloned.1.call-done) | data formatting | bytes 25165824 | tf_op jit(solution)/shard_map/all_gather | solution.py:61
  121.6 12.8 %copy.109 = bf16[96,8,16,512]{3,2,1,0:T(8,128)(2,1)} copy(bf16[96,8,16,512]{3,1,2,0:T(8,128)(2,1)} %bitcast.177) | data formatting | bytes 25165824
  134.4 17.5 %copy.90 = bf16[16,2,512,3,128]{4,2,3,1,0:T(8,128)(2,1)} copy(bf16[16,2,512,3,128]{2,0,4,3,1:T(8,128)(2,1)} %bitcast.178) | data formatting | bytes 25165824 | tf_op jit(solution)/shard_map/while | solution.py:75
  152.0 149.5 %while.20 = (s32[]{:T(128)}, f32[512,3]{0,1:T(4,128)S(1)}, f32[512,3]{0,1:T(4,128)S(1)}, f32[512,3,128]{0,2,1:T(8,128)S(1)}, f32[512,3]{0,1:T(4,128)S(1)}, /*ind...) while((s32[]{:T(128)}, f32[512,3]{0,1:T(4,128)S(1)}, ...), condition=%wide.region_9.10_spmd, body=%wide.region_4.9_spmd.sunk | while | flops 819474432 | bytes 25338080 | solution.py:75
  159.4 1.9 fusion.90
  168.8 1.9 fusion.90
  178.1 1.9 fusion.90
  185.6 1.9 fusion.91
  187.4 1.9 fusion.90
  196.8 1.9 fusion.90
  206.1 1.9 fusion.90
  215.5 1.9 fusion.90
  224.8 1.9 fusion.90
  234.2 1.9 fusion.90
  243.5 1.9 fusion.90
  252.8 1.9 fusion.90
  262.2 1.9 fusion.90
  271.5 1.9 fusion.90
  280.9 1.9 fusion.90
  290.2 1.9 fusion.90
  299.6 1.9 fusion.90
  303.4 7.5 %all-to-all-start.3 = ((bf16[512,3,128]{2,1,0:T(4,128)(2,1)}), bf16[512,3,128]{2,1,0:T(4,128)(2,1)S(1)}, u32[]{:S(2)}, u32[]{:S(2)}) async-start(bf16[512,3,128]{2,1,0:T(4,128)(2,1)} %divide_convert_fusion), calls=%async_computation.3 | async-start | bytes 1048576 | tf_op jit(solution)/shard_map/all_to_all | solution.py:81
  312.9 10.0 %all-to-all-done.3 = bf16[512,3,128]{2,1,0:T(4,128)(2,1)S(1)} async-done(((bf16[512,3,128]{2,1,0:T(4,128)(2,1)}), bf16[512,3,128]{2,1,0:T(4,128)(2,1)S(1)}, u32[]{:S(2)}, u32[]{:S(2)}) %all-to-all-start.3) | async-done | bytes 393248 | tf_op jit(solution)/shard_map/all_to_all | solution.py:81
  323.0 3.7 %all-to-all-start.2 = ((bf16[512,3,128]{2,1,0:T(4,128)(2,1)}), bf16[512,3,128]{2,1,0:T(4,128)(2,1)S(1)}, u32[]{:S(2)}, u32[]{:S(2)}) async-start(bf16[512,3,128]{2,1,0:T(4,128)(2,1)} %divide_convert_fusion.1), calls=%async_computation.2 | async-start | bytes 1048576 | tf_op jit(solution)/shard_map/all_to_all | solution.py:80
  328.1 9.3 %all-to-all-done.2 = bf16[512,3,128]{2,1,0:T(4,128)(2,1)S(1)} async-done(((bf16[512,3,128]{2,1,0:T(4,128)(2,1)}), bf16[512,3,128]{2,1,0:T(4,128)(2,1)S(1)}, u32[]{:S(2)}, u32[]{:S(2)}) %all-to-all-start.2) | async-done | bytes 393248 | tf_op jit(solution)/shard_map/all_to_all | solution.py:80
  338.2 10.5 %fusion.45 = bf16[64,3072]{1,0:T(8,128)(2,1)} fusion(bf16[64,3072]{1,0:T(8,128)(2,1)S(1)} %reshape.39, bf16[3072,3072]{1,0:T(8,128)(2,1)} %param.13, bf16[64,3072]{1,0:T(8,128)(2,1)S(1)} %copy-done.6, f32[3072]{0:T(1024)S(1)} %copy-done.7), kind=kOutput, calls=%fused_computation.44 | convolution fusion | flops 1208745984 | bytes 20066304 | tf_op jit(solution)/shard_map/dot_general | solution.py:84
  (155 shorter events, 128.4 us)
Async XLA Ops:
  7.2 97.8 %all-gather.2.cloned.1.call-start = ((), (), s32[]{:S(2)}) async-start(), calls=%async_computation.4 | async-start | bytes 13369344 | tf_op jit(solution)/shard_map/all_gather | solution.py:61
  7.9 9.8 %copy-start.5 = (bf16[64,9216]{1,0:T(8,128)(2,1)S(1)}, bf16[64,9216]{1,0:T(8,128)(2,1)}, u32[]{:S(2)}) copy-start(bf16[64,9216]{1,0:T(8,128)(2,1)} %param.9) | copy-start | bytes 3538948
  10.8 37.5 %all-to-all-start.1 = ((bf16[64,3,24,128]{3,0,1,2:T(8,128)(2,1)}), bf16[64,3,24,128]{3,0,1,2:T(8,128)(2,1)S(1)}, u32[]{:S(2)}, u32[]{:S(2)}) async-start(bf16[64,3,24,128]{3,0,1,2:T(8,128)(2,1)} %copy.82), calls=%async_computation.1 | async-start | bytes 2359296 | tf_op jit(solution)/shard_map/all_to_all | solution.py:47
  48.3 35.3 %all-to-all-start = ((bf16[64,3,24,128]{3,0,1,2:T(8,128)(2,1)}), bf16[64,3,24,128]{3,0,1,2:T(8,128)(2,1)}, u32[]{:S(2)}, u32[]{:S(2)}) async-start(bf16[64,3,24,128]{3,0,1,2:T(8,128)(2,1)} %copy.79), calls=%async_computation | async-start | bytes 2359296 | tf_op jit(solution)/shard_map/all_to_all | solution.py:48
  52.7 32.9 %copy-start.4 = (bf16[8,64,3,3,128]{4,1,0,3,2:T(8,128)(2,1)}, bf16[8,64,3,3,128]{4,1,0,3,2:T(8,128)(2,1)S(1)}, u32[]{:S(2)}) copy-start(bf16[8,64,3,3,128]{4,1,0,3,2:T(8,128)(2,1)S(1)} %copy.84) | copy-start | bytes 3538948
  85.0 4.0 %copy-start.3 = (bf16[8,64,3,3,128]{4,1,0,3,2:T(8,128)(2,1)}, bf16[8,64,3,3,128]{4,1,0,3,2:T(8,128)(2,1)S(1)}, u32[]{:S(2)}) copy-start(bf16[8,64,3,3,128]{4,1,0,3,2:T(8,128)(2,1)S(1)} %copy.81) | copy-start | bytes 3538948
  85.6 1.6 copy-start
  89.0 1.6 copy-start.2
  91.8 2.5 copy-start.1
  303.4 19.5 %all-to-all-start.3 = ((bf16[512,3,128]{2,1,0:T(4,128)(2,1)}), bf16[512,3,128]{2,1,0:T(4,128)(2,1)S(1)}, u32[]{:S(2)}, u32[]{:S(2)}) async-start(bf16[512,3,128]{2,1,0:T(4,128)(2,1)} %divide_convert_fusion), calls=%async_computation.3 | async-start | bytes 1048576 | tf_op jit(solution)/shard_map/all_to_all | solution.py:81
  312.9 25.3 %copy-start.6 = (bf16[64,3072]{1,0:T(8,128)(2,1)S(1)}, bf16[64,3072]{1,0:T(8,128)(2,1)}, u32[]{:S(2)}) copy-start(bf16[64,3072]{1,0:T(8,128)(2,1)} %param.11) | copy-start | bytes 1179652
  312.9 25.3 %copy-start.7 = (f32[3072]{0:T(1024)S(1)}, f32[3072]{0:T(1024)}, u32[]{:S(2)}) copy-start(f32[3072]{0:T(1024)} %param.12) | copy-start | bytes 36868
  323.0 14.5 %all-to-all-start.2 = ((bf16[512,3,128]{2,1,0:T(4,128)(2,1)}), bf16[512,3,128]{2,1,0:T(4,128)(2,1)S(1)}, u32[]{:S(2)}, u32[]{:S(2)}) async-start(bf16[512,3,128]{2,1,0:T(4,128)(2,1)} %divide_convert_fusion.1), calls=%async_computation.2 | async-start | bytes 1048576 | tf_op jit(solution)/shard_map/all_to_all | solution.py:80
Sparse Core Ops, SparseCore 0:
  9.6 95.2 all-gather.1
where the time goes:
time: 360 us; the launch traced here: 356 us
  matrix products  125 us (35%)
  waiting for transfers between devices  87.7 us (24%)
  local copies, waits for them, and re-layouts  72.4 us (20%)
  other arithmetic  23.4 us (6%)
  starting transfers between devices  22.4 us (6%)
  between operations  14.3 us (4%)
  loops' own time  10.8 us (3%)
    dot_general x34, matrix products, block_stats(): jnp.einsum('rhk,khd->rhd', shifted.astype(jnp.bfloat16), values, preferre...  62.2 us
    dot_general x34, matrix products, block_stats(): jnp.einsum('rhd,khd->rhk', queries, key_rows, preferred_element_type=jnp....  51.9 us
    all_to_all x1, waiting for transfers between devices, per_device(): lax.all_to_all(txt_split, 'head', split_axis=2, concat_axis=0, tiled=True)  30.9 us
    all_to_all x1, waiting for transfers between devices, per_device(): lax.all_to_all(img_split, 'head', split_axis=2, concat_axis=0, tiled=True)  29.1 us
    reduce_sum x33, other arithmetic, block_stats(): row_sum = jnp.sum(shifted, axis=2)  20 us
    while x7, local copies, waits for them, and re-layouts, per_device(): lax.scan(one_block, (image_init, text_init), (key_blocks, starts))  19.1 us
    unnamed x19, local copies, waits for them, and re-layouts  18.7 us
    all_gather x1, local copies, waits for them, and re-layouts, per_device(): shard_rows = lax.all_gather(stale_kv, 'patch', axis=1, tiled=True)  16.7 us
  transfers between devices with their start and end apart: 5, of which 5 were waited for; matrix products, arithmetic and copies ran while one was open for 5% of the time, Pallas kernels for 0%

commit v1 on v0

v1 whole, which is shorter than its diff:
```python
import math

import jax
import jax.numpy as jnp
from jax import lax
from jax.experimental import pallas as pl
from jax.experimental.pallas import tpu as pltpu
from jax.sharding import PartitionSpec as P

HD = 128
NH = 3
W3 = NH * HD
D = 3072
N_HEAD = 8
GR = 512
MINE = GR + 32
ROWS = 2 * MINE
LOG2E_SCALE = math.log2(math.e) / math.sqrt(HD)
MESH = pl.DeviceIdType.MESH
SLOTS = (1, 2, 6, 3, 7, 4, 5)


def pick(i, values):
    out = jnp.int32(values[-1])
    for n, value in enumerate(values[:-1]):
        out = jnp.where(i == n, jnp.int32(value), out)
    return out


def kernel(
    img, txt, stale, residual, gate, weight,
    out_img, out_txt,
    q_buf, tq, kv, fresh, tkv, acc, mx, wbuf, po, pr, ls, lr, fin, tfin, tattn, attn, total, res, gat, obuf,
    s_q, r_q, s_p, r_p, s_t, r_t, s_f, r_f, s_x, r_x, s_k, r_k, s_o, r_o, s_b, r_b, s_ta, r_ta, s_tb, r_tb, lsem, wsem,
):
    p = lax.axis_index("patch")
    h = lax.axis_index("head")
    z = p // 4
    x = (p // 2) % 2
    c = p % 2
    t = z * 2 + c
    sib = p + 1 - 2 * c
    part = p + 2 - 4 * x
    up = ((z + 1) % 4) * 4 + x * 2 + c
    down = ((z + 3) % 4) * 4 + x * 2 + c
    text_here = (h // 4) == x

    def rcopy(src, dst, ssem, rsem, to):
        return pltpu.make_async_remote_copy(
            src_ref=src, dst_ref=dst, send_sem=ssem, recv_sem=rsem, device_id=to, device_id_type=MESH
        )

    def peer(i):
        return (h + i) % N_HEAD

    def cols(base, head):
        return pl.ds(pl.multiple_of(base + head * W3, 128), W3)

    loads = [
        pltpu.make_async_copy(img.at[:, cols(0, h)], q_buf.at[pl.ds(pl.multiple_of(64 * h, 64), 64), :], lsem.at[0]),
        pltpu.make_async_copy(txt.at[pl.ds(pl.multiple_of(8 * t, 8), 8), cols(0, h)], tq.at[h], lsem.at[1]),
        pltpu.make_async_copy(stale, kv.at[0], lsem.at[2]),
        pltpu.make_async_copy(img.at[:, cols(D, h)], fresh.at[0, pl.ds(pl.multiple_of(64 * h, 64), 64), :], lsem.at[3]),
        pltpu.make_async_copy(img.at[:, cols(2 * D, h)], fresh.at[1, pl.ds(pl.multiple_of(64 * h, 64), 64), :], lsem.at[4]),
        pltpu.make_async_copy(residual, res, lsem.at[5]),
        pltpu.make_async_copy(gate, gat, lsem.at[6]),
    ]
    for one in loads:
        one.start()
    wloads = []
    for j in range(NH):
        for g in range(N_HEAD):
            one = pltpu.make_async_copy(
                weight.at[pl.ds((NH * g + j) * HD, HD), :], wbuf.at[j, pl.ds(g * HD, HD), :], wsem.at[j * N_HEAD + g]
            )
            wloads.append(one)
    text_rows = pl.ds(pl.multiple_of(64 * (h % 4), 64), 64)
    tlocal = [
        pltpu.make_async_copy(txt.at[:, cols(D * (1 + n), h)], tkv.at[n, text_rows, :], lsem.at[7 + n]) for n in range(2)
    ]

    @pl.when(text_here)
    def _():
        for one in tlocal:
            one.start()

    barrier = pltpu.get_barrier_semaphore()
    greeted = 0
    for i in range(1, N_HEAD):
        pl.semaphore_signal(barrier, inc=1, device_id=(p, peer(i)), device_id_type=MESH)
        greeted += 1
    for i in range(N_HEAD):
        pl.semaphore_signal(barrier, inc=1, device_id=(part, peer(i)), device_id_type=MESH)
        greeted += 1
    for i in range(1, 16):
        other = (p + i) % 16

        @pl.when(other != part)
        def _():
            pl.semaphore_signal(barrier, inc=1, device_id=(other, h), device_id_type=MESH)

    greeted += 14
    pl.semaphore_wait(barrier, greeted)

    own_rows = pl.ds(pl.multiple_of(64 * h, 64), 64)
    part_rows = pl.ds(pl.multiple_of(MINE + 64 * h, 32), 64)
    sends = []

    def q_copy(i):
        to = peer(i)
        return rcopy(img.at[:, cols(0, to)], q_buf.at[own_rows, :], s_q.at[i], r_q.at[h], (p, to))

    def p_copy(i):
        to = peer(i)
        return rcopy(img.at[:, cols(0, to)], q_buf.at[part_rows, :], s_p.at[i], r_p.at[h], (part, to))

    def t_copy(i):
        to = peer(i)
        return rcopy(
            txt.at[pl.ds(pl.multiple_of(8 * t, 8), 8), cols(0, to)], tq.at[h], s_t.at[i], r_t.at[h], (p, to)
        )

    def f_copy(i, n):
        to = peer(i)
        return rcopy(
            img.at[:, cols(D * (1 + n), to)], fresh.at[n, own_rows, :], s_f.at[n, i], r_f.at[n, h], (p, to)
        )

    def x_copy(i, n):
        to = peer(i)
        return rcopy(
            txt.at[:, cols(D * (1 + n), to)], tkv.at[n, text_rows, :], s_x.at[n, i], r_x.at[n, h % 4], (p, to)
        )

    def hs(j):
        return pl.ds(j * HD, HD)

    def k_copy(j, n):
        to, slot = ((sib, 1), (up, 2), (down, 6))[n]
        return rcopy(
            stale.at[:, :, hs(j)], kv.at[slot, :, :, hs(j)], s_k.at[j, n], r_k.at[j, slot], (to, h)
        )

    def z_forward(j):
        src = 2 + 4 * c
        to = ((z + 1 + 2 * c) % 4) * 4 + x * 2 + c
        return rcopy(kv.at[src, :, :, hs(j)], kv.at[4, :, :, hs(j)], s_k.at[j, 3], r_k.at[j, 4], (to, h))

    def sib_forward(j, slot, n):
        return rcopy(
            kv.at[slot, :, :, hs(j)], kv.at[slot + 1, :, :, hs(j)], s_k.at[j, 4 + n], r_k.at[j, slot + 1], (sib, h)
        )

    for i in range(1, N_HEAD):
        q_copy(i).start()
    for n in range(3):
        k_copy(0, n).start()
    for i in range(1, N_HEAD):
        t_copy(i).start()
    for i in range(N_HEAD):
        p_copy(i).start()
    for one in wloads:
        one.start()

    mx[...] = jnp.full_like(mx, -1e30)
    acc[...] = jnp.zeros_like(acc)

    def wait_block(dst, sem):
        rcopy(dst, dst, sem, sem, (p, h)).wait_recv()

    def rows_of(source):
        return pl.ds(64 * source, 64)

    loads[0].wait()
    for i in range(1, N_HEAD):
        source = peer(i)
        wait_block(q_buf.at[pl.ds(pl.multiple_of(64 * source, 64), 64), :], r_q.at[source])
    loads[1].wait()
    for i in range(1, N_HEAD):
        source = peer(i)
        wait_block(tq.at[source], r_t.at[source])
    mine_text = tq[pl.ds(4 * x, 4)].astype(jnp.float32).reshape(32, W3).astype(jnp.bfloat16)
    q_buf[GR:MINE, :] = mine_text
    other_text = tq[pl.ds(4 - 4 * x, 4)].astype(jnp.float32).reshape(32, W3).astype(jnp.bfloat16)
    q_buf[MINE + GR : ROWS, :] = other_text
    for i in range(N_HEAD):
        source = peer(i)
        wait_block(q_buf.at[pl.ds(pl.multiple_of(MINE + 64 * source, 32), 64), :], r_p.at[source])
    loads[2].wait()

    for i in range(1, N_HEAD):
        for n in range(2):
            f_copy(i, n).start()

    @pl.when(text_here)
    def _():
        for i in range(1, N_HEAD):
            for n in range(2):
                x_copy(i, n).start()

    def attend(j, first, count, keys, values):
        rows = slice(first, first + count)
        scores = lax.dot_general(
            q_buf[rows, hs(j)], keys, (((1,), (1,)), ((), ())), preferred_element_type=jnp.float32
        )
        old = mx[j, rows, :]
        new = jnp.maximum(old, jnp.max(scores, axis=1, keepdims=True) * LOG2E_SCALE)
        weights = jnp.exp2(scores * LOG2E_SCALE - new[:, :1]).astype(jnp.bfloat16)
        decay = jnp.exp2(old - new)
        mx[j, rows, :] = new
        wide = jnp.concatenate([values, jnp.ones_like(values)], axis=1)
        mixed = jnp.dot(weights, wide, preferred_element_type=jnp.float32)
        acc[j, rows, :HD] = acc[j, rows, :HD] * decay + mixed[:, :HD]
        acc[j, rows, HD:] = acc[j, rows, HD:] * decay + mixed[:, HD:]

    def finish_partner(j):
        rows = slice(MINE, ROWS)
        sums = acc[j, rows, HD:]
        po[j] = (acc[j, rows, :HD] / sums).astype(jnp.bfloat16)
        lse = mx[j, rows, :] + jnp.log2(sums)
        lse = jnp.concatenate([lse, jnp.zeros((640 - MINE, HD), jnp.float32)], axis=0)
        ls[j] = jnp.transpose(lse)[:8, :]

    def o_copy(j, n):
        if n == 0:
            return rcopy(po.at[j], pr.at[j], s_o.at[j, 0], r_o.at[j, 0], (part, h))
        return rcopy(ls.at[j], lr.at[j], s_o.at[j, 1], r_o.at[j, 1], (part, h))

    def b_copy(j, i):
        to = peer(i)
        return rcopy(
            fin.at[j, pl.ds(pl.multiple_of(64 * to, 64), 64), :],
            attn.at[j, :, pl.ds(pl.multiple_of(h * HD, HD), HD)],
            s_b.at[j, i], r_b.at[j, h], (p, to),
        )

    def b_local(j):
        return pltpu.make_async_copy(
            fin.at[j, own_rows, :], attn.at[j, :, pl.ds(pl.multiple_of(h * HD, HD), HD)], lsem.at[9 + j]
        )

    def combine(j):
        wait_block(pr.at[j], r_o.at[j, 0])
        wait_block(lr.at[j], r_o.at[j, 1])
        row = lr[j]
        theirs = jnp.transpose(jnp.concatenate([row] * 16, axis=0))[:MINE, :]
        mine = mx[j, :MINE, :]
        top = jnp.maximum(mine, theirs)
        a = jnp.exp2(mine - top)
        b = jnp.exp2(theirs - top)
        both = acc[j, :MINE, :HD] * a + pr[j].astype(jnp.float32) * b
        done = both / (acc[j, :MINE, HD:] * a + b)
        fin[j] = done[:GR].astype(jnp.bfloat16)
        tfin[:, :, j * HD : (j + 1) * HD] = done[GR:].reshape(4, 8, HD).astype(jnp.bfloat16)
        for i in range(1, N_HEAD):
            b_copy(j, i).start()
        b_local(j).start()

    def project(j):
        b_local(j).wait()
        for i in range(1, N_HEAD):
            source = peer(i)
            wait_block(attn.at[j, :, pl.ds(pl.multiple_of(source * HD, HD), HD)], r_b.at[j, source])
        for g in range(N_HEAD):
            wloads[j * N_HEAD + g].wait()
        rows = attn[j]

        def tile(n, _):
            part_cols = pl.ds(pl.multiple_of(n * 512, 512), 512)
            prod = jnp.dot(rows, wbuf[j, :, part_cols], preferred_element_type=jnp.float32)
            if j == 0:
                total[:, part_cols] = prod
            else:
                total[:, part_cols] = total[:, part_cols] + prod
            return 0

        lax.fori_loop(0, D // 512, tile, 0)

    for j in range(NH):
        attend(j, GR, ROWS - GR, kv[0, 0, :, hs(j)], kv[0, 1, :, hs(j)])

        def block(i, _, j=j):
            slot = pick(i, SLOTS)
            wait_block(kv.at[slot, :, :, hs(j)], r_k.at[j, slot])

            @pl.when(i == 1)
            def _():
                sib_forward(j, 2, 0).start()

                @pl.when(c == 0)
                def _():
                    z_forward(j).start()

                if j + 1 < NH:
                    k_copy(j + 1, 1).start()

            @pl.when(i == 2)
            def _():
                sib_forward(j, 6, 1).start()

                @pl.when(c == 1)
                def _():
                    z_forward(j).start()

                if j + 1 < NH:
                    k_copy(j + 1, 2).start()
                    k_copy(j + 1, 0).start()

            @pl.when(i == 5)
            def _():
                sib_forward(j, 4, 2).start()

            keys, values = kv[slot, 0, :, hs(j)], kv[slot, 1, :, hs(j)]
            attend(j, 0, MINE, keys, values)
            attend(j, MINE, MINE, keys, values)
            return 0

        lax.fori_loop(0, len(SLOTS), block, 0)
        if j == 0:
            for n in range(2):
                loads[3 + n].wait()
            for i in range(1, N_HEAD):
                source = peer(i)
                for n in range(2):
                    wait_block(fresh.at[n, pl.ds(pl.multiple_of(64 * source, 64), 64), :], r_f.at[n, source])
            for g in range(4):
                for n in range(2):

                    @pl.when(h == 4 * x + g)
                    def _():
                        tlocal[n].wait()

                    @pl.when(h != 4 * x + g)
                    def _():
                        wait_block(tkv.at[n, pl.ds(64 * g, 64), :], r_x.at[n, g])

        attend(j, 0, GR, fresh[0, :, hs(j)], fresh[1, :, hs(j)])
        keys, values = tkv[0, :, hs(j)], tkv[1, :, hs(j)]
        attend(j, 0, MINE, keys, values)
        attend(j, MINE, MINE, keys, values)
        finish_partner(j)
        for n in range(2):
            o_copy(j, n).start()
        if j >= 1:
            combine(j - 1)

    project(0)
    combine(2)

    def ta_copy(g):
        to = 4 * x + g
        return rcopy(
            tfin.at[g], tattn.at[:, cols(0, h)], s_ta.at[g], r_ta.at[h], (p, to)
        )

    def ta_local(g):
        return pltpu.make_async_copy(tfin.at[g], tattn.at[:, cols(0, h)], lsem.at[12])

    for g in range(4):

        @pl.when(h == 4 * x + g)
        def _():
            ta_local(g).start()

        @pl.when(h != 4 * x + g)
        def _():
            ta_copy(g).start()

    project(1)

    def tb_copy(i):
        other = (p + i) % 16
        return rcopy(tattn, out_txt.at[t], s_tb.at[i], r_tb.at[t], (other, h))

    tb_local = pltpu.make_async_copy(tattn, out_txt.at[t], lsem.at[13])

    @pl.when(text_here)
    def _():
        ta_local(0).wait()
        for i in range(1, N_HEAD):
            source = peer(i)
            wait_block(tattn.at[:, cols(0, source)], r_ta.at[source])
        for i in range(1, 16):
            tb_copy(i).start()
        tb_local.start()

    project(2)
    loads[5].wait()
    loads[6].wait()
    obuf[...] = (res[...].astype(jnp.float32) + gat[...] * total[...]).astype(jnp.bfloat16)
    out_copy = pltpu.make_async_copy(obuf, out_img, lsem.at[14])
    out_copy.start()

    for n in range(8):

        @pl.when(jnp.logical_and(text_here, t == n))
        def _():
            tb_local.wait()

        @pl.when(jnp.logical_not(jnp.logical_and(text_here, t == n)))
        def _():
            wait_block(out_txt.at[n], r_tb.at[n])

    for i in range(1, N_HEAD):
        q_copy(i).wait_send()
        t_copy(i).wait_send()
        for n in range(2):
            f_copy(i, n).wait_send()
        for j in range(NH):
            b_copy(j, i).wait_send()
    for i in range(N_HEAD):
        p_copy(i).wait_send()

    @pl.when(text_here)
    def _():
        for i in range(1, N_HEAD):
            for n in range(2):
                x_copy(i, n).wait_send()
        for i in range(1, 16):
            tb_copy(i).wait_send()

    for g in range(4):

        @pl.when(h != 4 * x + g)
        def _():
            ta_copy(g).wait_send()

    for j in range(NH):
        for n in range(3):
            k_copy(j, n).wait_send()
        z_forward(j).wait_send()
        for n, slot in enumerate((2, 6, 4)):
            sib_forward(j, slot, n).wait_send()
        for n in range(2):
            o_copy(j, n).wait_send()
    out_copy.wait()


def per_device(img_qkv, txt_qkv, stale_kv, residual, gate_scale, proj_weight):
    any_space = pl.BlockSpec(memory_space=pl.ANY)
    bf, f32 = jnp.bfloat16, jnp.float32
    dma = pltpu.SemaphoreType.DMA
    image_out, text_out = pl.pallas_call(
        kernel,
        out_shape=(jax.ShapeDtypeStruct((64, D), bf), jax.ShapeDtypeStruct((8, 8, D), bf)),
        in_specs=[any_space] * 6,
        out_specs=(any_space, any_space),
        scratch_shapes=[
            pltpu.VMEM((ROWS, W3), bf),
            pltpu.VMEM((8, 8, W3), bf),
            pltpu.VMEM((8, 2, GR, W3), bf),
            pltpu.VMEM((2, GR, W3), bf),
            pltpu.VMEM((2, 256, W3), bf),
            pltpu.VMEM((NH, ROWS, 2 * HD), f32),
            pltpu.VMEM((NH, ROWS, HD), f32),
            pltpu.VMEM((NH, N_HEAD * HD, D), bf),
            pltpu.VMEM((NH, MINE, HD), bf),
            pltpu.VMEM((NH, MINE, HD), bf),
            pltpu.VMEM((NH, 8, 640), f32),
            pltpu.VMEM((NH, 8, 640), f32),
            pltpu.VMEM((NH, GR, HD), bf),
            pltpu.VMEM((4, 8, W3), bf),
            pltpu.VMEM((8, D), bf),
            pltpu.VMEM((NH, 64, N_HEAD * HD), bf),
            pltpu.VMEM((64, D), f32),
            pltpu.VMEM((64, D), bf),
            pltpu.VMEM((1, D), f32),
            pltpu.VMEM((64, D), bf),
            dma((8,)), dma((8,)),
            dma((8,)), dma((8,)),
            dma((8,)), dma((8,)),
            dma((2, 8)), dma((2, 8)),
            dma((2, 8)), dma((2, 4)),
            dma((NH, 7)), dma((NH, 8)),
            dma((NH, 2)), dma((NH, 2)),
            dma((NH, 8)), dma((NH, 8)),
            dma((4,)), dma((8,)),
            dma((16,)), dma((8,)),
            dma((15,)), dma((24,)),
        ],
        compiler_params=pltpu.CompilerParams(
            collective_id=0, has_side_effects=True, vmem_limit_bytes=62 * 1024 * 1024
        ),
    )(img_qkv, txt_qkv, stale_kv, residual, gate_scale.reshape(1, D), proj_weight)
    return image_out, text_out.reshape(64, D)


def solution(mesh):
    return jax.shard_map(
        per_device,
        mesh=mesh,
        in_specs=(
            P(("patch", "head"), None),
            P("head", None),
            P(None, "patch", "head"),
            P(("patch", "head"), None),
            P(),
            P(),
        ),
        out_specs=(P(("patch", "head"), None), P("head", None)),
        check_vma=False,
    )
```

time: 360 us -> 95.9 us (0.27)
  the two profiles are of different devices: /device:TPU:96 before, /device:TPU:3 now
where the time goes in v1:
time: 95.9 us; the launch traced here: 95.7 us
  Pallas kernels  91.5 us (95%)
  local copies, waits for them, and re-layouts  3.53 us (4%)
    pallas_call x1, Pallas kernels, per_device(): pl.pallas_call(kernel, out_shape=(jax.ShapeDtypeStruct((64, D), bf), jax....  91.5 us
    unnamed x2, local copies, waits for them, and re-layouts  3.53 us

profile of v1, /device:TPU:3, one launch (start us, length us, event | category | flops | bytes accessed | tf_op | source)
XLA Modules:
  0.0 95.7 jit_solution(9906790024364138577)
XLA Ops:
  0.6 91.5 %shard_map.77 = (bf16[64,3072]{1,0:T(8,128)(2,1)}, bf16[8,8,3072]{2,1,0:T(8,128)(2,1)}) custom-call(bf16[64,9216]{1,0:T(8,128)(2,1)} %img.1, bf16[64,9216]{1,0:T(8,128)(2,1)} %txt.1, bf16[2,512,384]{2,1,0:T(8,128)(2,1)} %stale.1, bf16[64,3072]{1,0:T(8,128)(2,1)} %residual.1, f32[1,3072]{1,0:T(1,128)} %bitcast.3, bf16[3072,3072]{1,0:T(8,128)(2,1)} %weight.1), custom_call_target="tpu_custom_call" | custom-call | tf_op jit(solution)/shard_map/pallas_call | solution.py:443
  92.1 1.8 %copy.10 = bf16[64,3072]{1,0:T(8,128)(2,1)} copy(bf16[64,3072]{1,0:T(8,128)(2,1)} %get-tuple-element.8) | data formatting | bytes 786432
  93.9 1.8 %copy.11 = bf16[64,3072]{1,0:T(8,128)(2,1)} copy(bf16[64,3072]{1,0:T(8,128)(2,1)} %bitcast.2) | data formatting | bytes 786432
